TPU v7x, 512 devices: a whole 4x8x8 slice. The times are simulated.
512 devices in a mesh: blk: 128 (over y, z, core), rep: 4 (over x).
Axes of the slice: x: 4, y: 8, z: 8, core: 2. Of those that a mesh axis runs over, the one named last changes fastest.
Arguments:
- features: bfloat16 [65536, 256], P('blk'), may hold values from -6 to 6
- targets: bfloat16 [65536, 128], P('blk', 'rep'), may hold values from -6 to 6
- conditioning: int32 [512, 2], replicated, may hold values from 0 to 511, as said below
- block_slot: int32 [512], replicated, may hold values from 0 to 511, as said below
Outputs:
- whitened: float32 [65536, 128], P('blk', 'rep')
- grad_features: float32 [65536, 256], P('blk', 'rep')
- grad_targets: float32 [65536, 128], P('blk', 'rep')
Inputs may be any that keep to these rules, and one draw needn't show every extreme that they name: `conditioning`: row b lists 2 different blocks among b - 1, b - 2, ..., b - 3, taken modulo 512. `block_slot`: A permutation that keeps each aligned pair of slots 2i, 2i + 1 holding blocks 2i and 2i + 1, in either order; it is its own inverse.
All inputs are finite; a program needn't handle non-finite values.
Results may differ from a plain program's by a relative error of at most 0.0003.
Values may be sent and summed in bfloat16 or wider, within the bound.
No kernel may reach another device: no remote copies, remote signals or barrier semaphores. Data moves between devices by JAX's collectives and lax.ppermute only.
A program may use at most 64 MiB of HBM per device.

v0:
```python
import jax
import jax.numpy as jnp
from jax import lax
from jax.sharding import PartitionSpec as P

F = 256
PTS = 128
NCOND = 2
REACH = 3


linear_scale = 1.0
gauss_scale = 1.5
nugget = 0.1


def passed_along(value, axis, steps):
    count = lax.axis_size(axis)
    pairs = [(source, (source + steps) % count) for source in range(count)]
    return lax.ppermute(value, axis, pairs)


def block_loss(gram_matrix, values):
    points = gram_matrix.shape[0]
    squares = jnp.diagonal(gram_matrix)
    distance = squares[:, None] + squares[None, :] - 2.0 * gram_matrix
    kernel = (
        linear_scale * gram_matrix / F
        + gauss_scale * jnp.exp(-distance / (2.0 * F))
        + nugget * jnp.eye(points, dtype=gram_matrix.dtype)
    )
    factor = jnp.linalg.cholesky(kernel)
    solved = jax.scipy.linalg.solve_triangular(factor, values, lower=True)
    whitened = solved[points - PTS :]
    tail_diag = jnp.diagonal(factor)[points - PTS :]
    total_loss = 0.5 * jnp.sum(whitened * whitened) + values.shape[1] * jnp.sum(jnp.log(tail_diag))
    return (total_loss, whitened)


def block_grads(points, values):
    gram_matrix = jnp.dot(points, points.T, preferred_element_type=jnp.float32)
    total_loss, pullback, whitened = jax.vjp(block_loss, gram_matrix, values, has_aux=True)
    grad_gram, grad_values = pullback(jnp.ones_like(total_loss))
    grad_points = jnp.dot(
        grad_gram + grad_gram.T, points.astype(jnp.float32), precision=lax.Precision.HIGHEST
    )
    return (whitened, grad_points, grad_values)


def per_device(features, targets, conditioning, block_slot):
    rows_dev = features.shape[0]
    feat_width = features.shape[1]
    target_cols = targets.shape[1]
    blocks = rows_dev // PTS
    total_blocks = block_slot.shape[0]
    behind = (REACH + 1 + blocks) // blocks
    position = lax.axis_index("blk")
    slabs = {0: (features, targets)}
    for offset in range(-behind, 2):
        if offset != 0:
            slabs[offset] = passed_along((features, targets), "blk", -offset)
    window_features = jnp.concatenate([slabs[offset][0] for offset in range(-behind, 2)], axis=0)
    window_targets = jnp.concatenate([slabs[offset][1] for offset in range(-behind, 2)], axis=0)
    span_rows = window_features.shape[0]
    start_slot = (position - behind) * blocks % total_blocks

    def add_block(local_block, state_now):
        grad_window, target_window, whitened_all = state_now
        own_slot = position * blocks + local_block
        block_id = lax.dynamic_index_in_dim(block_slot, own_slot, 0, keepdims=False)
        listed = lax.dynamic_index_in_dim(conditioning, block_id, 0, keepdims=False)
        members = jnp.concatenate([listed, block_id[None]])
        window_pos = (jnp.take(block_slot, members) - start_slot) % total_blocks
        points = jnp.concatenate(
            [
                lax.dynamic_slice_in_dim(window_features, window_pos[member] * PTS, PTS, 0)
                for member in range(NCOND + 1)
            ],
            axis=0,
        )
        values = jnp.concatenate(
            [
                lax.dynamic_slice_in_dim(window_targets, window_pos[member] * PTS, PTS, 0)
                for member in range(NCOND + 1)
            ],
            axis=0,
        ).astype(jnp.float32)
        whitened, grad_points, grad_values = block_grads(points, values)
        for member in range(NCOND + 1):
            first_row = window_pos[member] * PTS
            grad_window = lax.dynamic_update_slice_in_dim(
                grad_window,
                lax.dynamic_slice_in_dim(grad_window, first_row, PTS, 0)
                + grad_points[member * PTS : (member + 1) * PTS],
                first_row,
                0,
            )
            target_window = lax.dynamic_update_slice_in_dim(
                target_window,
                lax.dynamic_slice_in_dim(target_window, first_row, PTS, 0)
                + grad_values[member * PTS : (member + 1) * PTS],
                first_row,
                0,
            )
        whitened_all = lax.dynamic_update_slice_in_dim(
            whitened_all, whitened, (local_block * PTS).astype(jnp.int32), 0
        )
        return (grad_window, target_window, whitened_all)

    initial = (
        jnp.zeros((span_rows, feat_width), jnp.float32),
        jnp.zeros((span_rows, target_cols), jnp.float32),
        jnp.zeros((rows_dev, target_cols), jnp.float32),
    )
    grad_window, target_window, whitened_all = lax.fori_loop(0, blocks, add_block, initial)
    grad_slabs = grad_window.reshape(behind + 2, rows_dev, feat_width)
    target_slabs = target_window.reshape(behind + 2, rows_dev, target_cols)
    grad_targets = target_slabs[behind]
    summed = grad_slabs[behind]
    for offset in range(-behind, 2):
        if offset != 0:
            arrived = passed_along(
                (grad_slabs[offset + behind], target_slabs[offset + behind]), "blk", offset
            )
            summed = summed + arrived[0]
            grad_targets = grad_targets + arrived[1]
    grad_features = lax.psum_scatter(summed, "rep", scatter_dimension=1, tiled=True)
    return (whitened_all, grad_features, grad_targets)


def solution(mesh):
    in_specs = (P("blk", None), P("blk", "rep"), P(), P())
    out_specs = (P("blk", "rep"), P("blk", "rep"), P("blk", "rep"))
    return jax.shard_map(
        per_device, mesh=mesh, in_specs=in_specs, out_specs=out_specs, check_vma=False
    )
```

profile of v0, /device:TPU:16, one launch (start us, length us, event | category | flops | bytes accessed | tf_op | source)
XLA Modules:
  0.0 982.8 jit_solution(1396723652652441422)
XLA Ops:
  39.4 884.8 %while.27 = (s32[]{:T(128)}, f32[2048,256]{1,0:T(8,128)}, f32[2048,32]{0,1:T(8,128)}, f32[512,32]{0,1:T(8,128)}, s32[]{:T(128)}, /*index=5*/s32[512]{0:T(512)S(1...) while((s32[]{:T(128)}, f32[2048,256]{1,0:T(8,128)}, ...), condition=%wide.region_11.14_spmd, body=%wide.region_0.13_spmd.sunk | while | flops 2433738496 | bytes 54162616 | solution.py:115
  77.6 11.7 %cholesky.320 = f32[128,128]{1,0:T(8,128)S(1)} custom-call(f32[128,128]{1,0:T(8,128)S(1)} %cholesky.319), custom_call_target="Cholesky" | custom-call | tf_op jit(solution)/shard_map/while/body/eval_jaxpr/jvp(jit(cholesky))/cholesky | solution.py:32
  89.3 9.8 custom-call.109
  99.7 11.7 %cholesky.323 = f32[128,128]{1,0:T(8,128)S(1)} custom-call(f32[128,128]{1,0:T(8,128)S(1)} %cholesky.322), custom_call_target="Cholesky" | custom-call | tf_op jit(solution)/shard_map/while/body/eval_jaxpr/jvp(jit(cholesky))/cholesky | solution.py:32
  124.9 11.7 %cholesky.324 = f32[128,128]{1,0:T(8,128)S(1)} custom-call(f32[128,128]{1,0:T(8,128)S(1)} %convolution_subtract_fusion.21), custom_call_target="Cholesky" | custom-call | tf_op jit(solution)/shard_map/while/body/eval_jaxpr/jvp(jit(cholesky))/cholesky | solution.py:32
  144.5 29.5 %custom-call.111 = f32[3,128,128]{1,2,0:T(8,128)S(1)} custom-call(f32[3,128,128]{2,1,0:T(8,128)S(1)} %get-tuple-element.630), custom_call_target="InvertDiagBlocksLowerTriangular" | custom-call | tf_op jit(solution)/shard_map/while/body/eval_jaxpr/transpose(jvp(jit(_solve_triangular)))/triangular_solve/custom-call.0 | solution.py:33
  185.8 21.1 %scatter_fusion = f32[384,384]{1,0:T(8,128)S(1)} fusion(f32[384,384]{1,0:T(8,128)S(1)} %copy.147, s32[384]{0:T(512)S(1)} %get-tuple-element.636, f32[384]{0:T(512)S(1)} %pad.262), kind=kCustom, calls=%fused_computation.3.clone.1 | custom fusion | flops 384 | bytes 7680 | tf_op jit(solution)/shard_map/while/body/eval_jaxpr/transpose(jvp(jit(diagonal)))/cond/branch_0_fun/scatter-add | solution.py:35
  214.7 29.5 %custom-call.112 = f32[3,128,128]{1,2,0:T(8,128)S(1)} custom-call(f32[3,128,128]{2,1,0:T(8,128)S(1)} %get-tuple-element.638), custom_call_target="InvertDiagBlocksLowerTriangular" | custom-call | tf_op jit(solution)/shard_map/while/body/eval_jaxpr/transpose(jvp(jit(cholesky)))/triangular_solve | solution.py:32
  251.1 21.1 %scatter_fusion.1 = f32[384,384]{1,0:T(8,128)S(1)} fusion(f32[384,384]{1,0:T(8,128)S(1)} %add_multiply_fusion.2, s32[384]{0:T(512)S(1)} %get-tuple-element.636, f32[384]{0:T(512)S(1)} %negate_add_fusion.2), kind=kCustom, calls=%fused_computation.4.clone.1 | custom fusion | flops 384 | bytes 7680 | tf_op jit(solution)/shard_map/while/body/eval_jaxpr/transpose(jvp(jit(diagonal)))/cond/branch_0_fun/scatter-add | solution.py:35
  292.5 11.7 %cholesky.320 = f32[128,128]{1,0:T(8,128)S(1)} custom-call(f32[128,128]{1,0:T(8,128)S(1)} %cholesky.319), custom_call_target="Cholesky" | custom-call | tf_op jit(solution)/shard_map/while/body/eval_jaxpr/jvp(jit(cholesky))/cholesky | solution.py:32
  314.6 11.7 %cholesky.323 = f32[128,128]{1,0:T(8,128)S(1)} custom-call(f32[128,128]{1,0:T(8,128)S(1)} %cholesky.322), custom_call_target="Cholesky" | custom-call | tf_op jit(solution)/shard_map/while/body/eval_jaxpr/jvp(jit(cholesky))/cholesky | solution.py:32
  339.8 11.7 %cholesky.324 = f32[128,128]{1,0:T(8,128)S(1)} custom-call(f32[128,128]{1,0:T(8,128)S(1)} %convolution_subtract_fusion.21), custom_call_target="Cholesky" | custom-call | tf_op jit(solution)/shard_map/while/body/eval_jaxpr/jvp(jit(cholesky))/cholesky | solution.py:32
  359.4 29.5 %custom-call.111 = f32[3,128,128]{1,2,0:T(8,128)S(1)} custom-call(f32[3,128,128]{2,1,0:T(8,128)S(1)} %get-tuple-element.630), custom_call_target="InvertDiagBlocksLowerTriangular" | custom-call | tf_op jit(solution)/shard_map/while/body/eval_jaxpr/transpose(jvp(jit(_solve_triangular)))/triangular_solve/custom-call.0 | solution.py:33
  400.7 21.1 %scatter_fusion = f32[384,384]{1,0:T(8,128)S(1)} fusion(f32[384,384]{1,0:T(8,128)S(1)} %copy.147, s32[384]{0:T(512)S(1)} %get-tuple-element.636, f32[384]{0:T(512)S(1)} %pad.262), kind=kCustom, calls=%fused_computation.3.clone.1 | custom fusion | flops 384 | bytes 7680 | tf_op jit(solution)/shard_map/while/body/eval_jaxpr/transpose(jvp(jit(diagonal)))/cond/branch_0_fun/scatter-add | solution.py:35
  429.6 29.5 %custom-call.112 = f32[3,128,128]{1,2,0:T(8,128)S(1)} custom-call(f32[3,128,128]{2,1,0:T(8,128)S(1)} %get-tuple-element.638), custom_call_target="InvertDiagBlocksLowerTriangular" | custom-call | tf_op jit(solution)/shard_map/while/body/eval_jaxpr/transpose(jvp(jit(cholesky)))/triangular_solve | solution.py:32
  466.0 21.1 %scatter_fusion.1 = f32[384,384]{1,0:T(8,128)S(1)} fusion(f32[384,384]{1,0:T(8,128)S(1)} %add_multiply_fusion.2, s32[384]{0:T(512)S(1)} %get-tuple-element.636, f32[384]{0:T(512)S(1)} %negate_add_fusion.2), kind=kCustom, calls=%fused_computation.4.clone.1 | custom fusion | flops 384 | bytes 7680 | tf_op jit(solution)/shard_map/while/body/eval_jaxpr/transpose(jvp(jit(diagonal)))/cond/branch_0_fun/scatter-add | solution.py:35
  507.4 11.7 %cholesky.320 = f32[128,128]{1,0:T(8,128)S(1)} custom-call(f32[128,128]{1,0:T(8,128)S(1)} %cholesky.319), custom_call_target="Cholesky" | custom-call | tf_op jit(solution)/shard_map/while/body/eval_jaxpr/jvp(jit(cholesky))/cholesky | solution.py:32
  529.5 11.7 %cholesky.323 = f32[128,128]{1,0:T(8,128)S(1)} custom-call(f32[128,128]{1,0:T(8,128)S(1)} %cholesky.322), custom_call_target="Cholesky" | custom-call | tf_op jit(solution)/shard_map/while/body/eval_jaxpr/jvp(jit(cholesky))/cholesky | solution.py:32
  554.7 11.7 %cholesky.324 = f32[128,128]{1,0:T(8,128)S(1)} custom-call(f32[128,128]{1,0:T(8,128)S(1)} %convolution_subtract_fusion.21), custom_call_target="Cholesky" | custom-call | tf_op jit(solution)/shard_map/while/body/eval_jaxpr/jvp(jit(cholesky))/cholesky | solution.py:32
  574.3 29.5 %custom-call.111 = f32[3,128,128]{1,2,0:T(8,128)S(1)} custom-call(f32[3,128,128]{2,1,0:T(8,128)S(1)} %get-tuple-element.630), custom_call_target="InvertDiagBlocksLowerTriangular" | custom-call | tf_op jit(solution)/shard_map/while/body/eval_jaxpr/transpose(jvp(jit(_solve_triangular)))/triangular_solve/custom-call.0 | solution.py:33
  615.6 21.1 %scatter_fusion = f32[384,384]{1,0:T(8,128)S(1)} fusion(f32[384,384]{1,0:T(8,128)S(1)} %copy.147, s32[384]{0:T(512)S(1)} %get-tuple-element.636, f32[384]{0:T(512)S(1)} %pad.262), kind=kCustom, calls=%fused_computation.3.clone.1 | custom fusion | flops 384 | bytes 7680 | tf_op jit(solution)/shard_map/while/body/eval_jaxpr/transpose(jvp(jit(diagonal)))/cond/branch_0_fun/scatter-add | solution.py:35
  644.5 29.5 %custom-call.112 = f32[3,128,128]{1,2,0:T(8,128)S(1)} custom-call(f32[3,128,128]{2,1,0:T(8,128)S(1)} %get-tuple-element.638), custom_call_target="InvertDiagBlocksLowerTriangular" | custom-call | tf_op jit(solution)/shard_map/while/body/eval_jaxpr/transpose(jvp(jit(cholesky)))/triangular_solve | solution.py:32
  680.9 21.1 %scatter_fusion.1 = f32[384,384]{1,0:T(8,128)S(1)} fusion(f32[384,384]{1,0:T(8,128)S(1)} %add_multiply_fusion.2, s32[384]{0:T(512)S(1)} %get-tuple-element.636, f32[384]{0:T(512)S(1)} %negate_add_fusion.2), kind=kCustom, calls=%fused_computation.4.clone.1 | custom fusion | flops 384 | bytes 7680 | tf_op jit(solution)/shard_map/while/body/eval_jaxpr/transpose(jvp(jit(diagonal)))/cond/branch_0_fun/scatter-add | solution.py:35
  722.3 11.7 %cholesky.320 = f32[128,128]{1,0:T(8,128)S(1)} custom-call(f32[128,128]{1,0:T(8,128)S(1)} %cholesky.319), custom_call_target="Cholesky" | custom-call | tf_op jit(solution)/shard_map/while/body/eval_jaxpr/jvp(jit(cholesky))/cholesky | solution.py:32
  734.0 9.8 custom-call.109
  744.4 11.7 %cholesky.323 = f32[128,128]{1,0:T(8,128)S(1)} custom-call(f32[128,128]{1,0:T(8,128)S(1)} %cholesky.322), custom_call_target="Cholesky" | custom-call | tf_op jit(solution)/shard_map/while/body/eval_jaxpr/jvp(jit(cholesky))/cholesky | solution.py:32
  769.6 11.7 %cholesky.324 = f32[128,128]{1,0:T(8,128)S(1)} custom-call(f32[128,128]{1,0:T(8,128)S(1)} %convolution_subtract_fusion.21), custom_call_target="Cholesky" | custom-call | tf_op jit(solution)/shard_map/while/body/eval_jaxpr/jvp(jit(cholesky))/cholesky | solution.py:32
  789.2 29.5 %custom-call.111 = f32[3,128,128]{1,2,0:T(8,128)S(1)} custom-call(f32[3,128,128]{2,1,0:T(8,128)S(1)} %get-tuple-element.630), custom_call_target="InvertDiagBlocksLowerTriangular" | custom-call | tf_op jit(solution)/shard_map/while/body/eval_jaxpr/transpose(jvp(jit(_solve_triangular)))/triangular_solve/custom-call.0 | solution.py:33
  830.5 21.1 %scatter_fusion = f32[384,384]{1,0:T(8,128)S(1)} fusion(f32[384,384]{1,0:T(8,128)S(1)} %copy.147, s32[384]{0:T(512)S(1)} %get-tuple-element.636, f32[384]{0:T(512)S(1)} %pad.262), kind=kCustom, calls=%fused_computation.3.clone.1 | custom fusion | flops 384 | bytes 7680 | tf_op jit(solution)/shard_map/while/body/eval_jaxpr/transpose(jvp(jit(diagonal)))/cond/branch_0_fun/scatter-add | solution.py:35
  859.5 29.5 %custom-call.112 = f32[3,128,128]{1,2,0:T(8,128)S(1)} custom-call(f32[3,128,128]{2,1,0:T(8,128)S(1)} %get-tuple-element.638), custom_call_target="InvertDiagBlocksLowerTriangular" | custom-call | tf_op jit(solution)/shard_map/while/body/eval_jaxpr/transpose(jvp(jit(cholesky)))/triangular_solve | solution.py:32
  895.9 21.1 %scatter_fusion.1 = f32[384,384]{1,0:T(8,128)S(1)} fusion(f32[384,384]{1,0:T(8,128)S(1)} %add_multiply_fusion.2, s32[384]{0:T(512)S(1)} %get-tuple-element.636, f32[384]{0:T(512)S(1)} %negate_add_fusion.2), kind=kCustom, calls=%fused_computation.4.clone.1 | custom fusion | flops 384 | bytes 7680 | tf_op jit(solution)/shard_map/while/body/eval_jaxpr/transpose(jvp(jit(diagonal)))/cond/branch_0_fun/scatter-add | solution.py:35
  962.0 13.7 %reduce-scatter.2.cloned.1.call-done = f32[512,64]{0,1:T(8,128)} async-done(((f32[512,256]{0,1:T(8,128)}), f32[512,64]{0,1:T(8,128)}) %reduce-scatter.2.cloned.1.call-update) | async-done | bytes 131088 | tf_op jit(solution)/shard_map/reduce_scatter | solution.py:127
  (599 shorter events, 387.8 us)
Async XLA Ops:
  7.2 968.6 %reduce-scatter.2.cloned.1.call-start = ((), (), s32[]{:S(2)}) async-start(), calls=%async_computation.1 | async-start | bytes 655360 | tf_op jit(solution)/shard_map/reduce_scatter | solution.py:127
  7.2 18.2 %collective-permute-start.3 = (bf16[512,32]{0,1:T(8,128)(2,1)}, bf16[512,32]{0,1:T(8,128)(2,1)S(1)}, u32[]{:S(2)}, u32[]{:S(2)}) collective-permute-start(bf16[512,32]{0,1:T(8,128)(2,1)} %param.10), channel_id=1, source_target_pairs={{0,8},{4,12},{8,16},{12,20},{16,24},{20,28},{24,32},{28,36},{32,40... | collective-permute-start | bytes 98312 | tf_op jit(solution)/shard_map/ppermute | solution.py:20
  11.5 23.0 %collective-permute-start = (bf16[512,256]{1,0:T(8,128)(2,1)}, bf16[512,256]{1,0:T(8,128)(2,1)S(1)}, u32[]{:S(2)}, u32[]{:S(2)}) collective-permute-start(bf16[512,256]{1,0:T(8,128)(2,1)} %param.9), channel_id=1, source_target_pairs={{0,8},{4,12},{8,16},{12,20},{16,24},{20,28},{24,32},{28,36},{32,40... | collective-permute-start | bytes 786440 | tf_op jit(solution)/shard_map/ppermute | solution.py:20
  15.8 18.7 %collective-permute-start.1 = (bf16[512,256]{1,0:T(8,128)(2,1)}, bf16[512,256]{1,0:T(8,128)(2,1)S(1)}, u32[]{:S(2)}, u32[]{:S(2)}) collective-permute-start(bf16[512,256]{1,0:T(8,128)(2,1)} %param.9), channel_id=1, source_target_pairs={{0,4},{4,8},{8,12},{12,16},{16,20},{20,24},{24,28},{28,32},{32,36}... | collective-permute-start | bytes 786440 | tf_op jit(solution)/shard_map/ppermute | solution.py:20
  17.7 16.8 %collective-permute-start.2 = (bf16[512,256]{1,0:T(8,128)(2,1)}, bf16[512,256]{1,0:T(8,128)(2,1)S(1)}, u32[]{:S(2)}, u32[]{:S(2)}) collective-permute-start(bf16[512,256]{1,0:T(8,128)(2,1)} %param.9), channel_id=1, source_target_pairs={{0,508},{4,0},{8,4},{12,8},{16,12},{20,16},{24,20},{28,24},{32,28}... | collective-permute-start | bytes 786440 | tf_op jit(solution)/shard_map/ppermute | solution.py:20
  23.5 9.3 collective-permute-start.4
  25.4 7.7 collective-permute-start.5
  34.5 4.9 copy-start
  71.7 0.9 copy-start.5
  251.1 21.4 %copy-start.2 = (bf16[128,256]{1,0:T(8,128)(2,1)S(1)}, bf16[128,256]{1,0:T(8,128)(2,1)}, u32[]{:S(2)}) copy-start(bf16[128,256]{1,0:T(8,128)(2,1)} %copy-done.1) | copy-start | bytes 196612 | tf_op jit(solution)/shard_map/while
  251.1 21.4 %copy-start.4 = (bf16[128,256]{1,0:T(8,128)(2,1)S(1)}, bf16[128,256]{1,0:T(8,128)(2,1)}, u32[]{:S(2)}) copy-start(bf16[128,256]{1,0:T(8,128)(2,1)} %copy-done.3) | copy-start | bytes 196612 | tf_op jit(solution)/shard_map/while
  251.1 21.4 %copy-start.6 = (bf16[128,256]{1,0:T(8,128)(2,1)S(1)}, bf16[128,256]{1,0:T(8,128)(2,1)}, u32[]{:S(2)}) copy-start(bf16[128,256]{1,0:T(8,128)(2,1)} %copy-done.5) | copy-start | bytes 196612 | tf_op jit(solution)/shard_map/while
  286.6 0.9 copy-start.3
  286.6 0.9 copy-start.5
  466.0 21.4 %copy-start.2 = (bf16[128,256]{1,0:T(8,128)(2,1)S(1)}, bf16[128,256]{1,0:T(8,128)(2,1)}, u32[]{:S(2)}) copy-start(bf16[128,256]{1,0:T(8,128)(2,1)} %copy-done.1) | copy-start | bytes 196612 | tf_op jit(solution)/shard_map/while
  466.0 21.4 %copy-start.4 = (bf16[128,256]{1,0:T(8,128)(2,1)S(1)}, bf16[128,256]{1,0:T(8,128)(2,1)}, u32[]{:S(2)}) copy-start(bf16[128,256]{1,0:T(8,128)(2,1)} %copy-done.3) | copy-start | bytes 196612 | tf_op jit(solution)/shard_map/while
  466.0 21.4 %copy-start.6 = (bf16[128,256]{1,0:T(8,128)(2,1)S(1)}, bf16[128,256]{1,0:T(8,128)(2,1)}, u32[]{:S(2)}) copy-start(bf16[128,256]{1,0:T(8,128)(2,1)} %copy-done.5) | copy-start | bytes 196612 | tf_op jit(solution)/shard_map/while
  501.5 0.9 copy-start.5
  680.9 21.4 %copy-start.2 = (bf16[128,256]{1,0:T(8,128)(2,1)S(1)}, bf16[128,256]{1,0:T(8,128)(2,1)}, u32[]{:S(2)}) copy-start(bf16[128,256]{1,0:T(8,128)(2,1)} %copy-done.1) | copy-start | bytes 196612 | tf_op jit(solution)/shard_map/while
  680.9 21.4 %copy-start.4 = (bf16[128,256]{1,0:T(8,128)(2,1)S(1)}, bf16[128,256]{1,0:T(8,128)(2,1)}, u32[]{:S(2)}) copy-start(bf16[128,256]{1,0:T(8,128)(2,1)} %copy-done.3) | copy-start | bytes 196612 | tf_op jit(solution)/shard_map/while
  680.9 21.4 %copy-start.6 = (bf16[128,256]{1,0:T(8,128)(2,1)S(1)}, bf16[128,256]{1,0:T(8,128)(2,1)}, u32[]{:S(2)}) copy-start(bf16[128,256]{1,0:T(8,128)(2,1)} %copy-done.5) | copy-start | bytes 196612 | tf_op jit(solution)/shard_map/while
  716.4 0.9 copy-start.5
  895.8 21.4 %copy-start.2 = (bf16[128,256]{1,0:T(8,128)(2,1)S(1)}, bf16[128,256]{1,0:T(8,128)(2,1)}, u32[]{:S(2)}) copy-start(bf16[128,256]{1,0:T(8,128)(2,1)} %copy-done.1) | copy-start | bytes 196612 | tf_op jit(solution)/shard_map/while
  895.8 21.4 %copy-start.4 = (bf16[128,256]{1,0:T(8,128)(2,1)S(1)}, bf16[128,256]{1,0:T(8,128)(2,1)}, u32[]{:S(2)}) copy-start(bf16[128,256]{1,0:T(8,128)(2,1)} %copy-done.3) | copy-start | bytes 196612 | tf_op jit(solution)/shard_map/while
  895.8 21.4 %copy-start.6 = (bf16[128,256]{1,0:T(8,128)(2,1)S(1)}, bf16[128,256]{1,0:T(8,128)(2,1)}, u32[]{:S(2)}) copy-start(bf16[128,256]{1,0:T(8,128)(2,1)} %copy-done.5) | copy-start | bytes 196612 | tf_op jit(solution)/shard_map/while
  926.3 21.4 %copy-start.7 = (f32[2048,32]{0,1:T(8,128)S(1)}, f32[2048,32]{0,1:T(8,128)}, u32[]{:S(2)}) copy-start(f32[2048,32]{0,1:T(8,128)} %get-tuple-element.292) | copy-start | bytes 786436
  926.3 15.9 %collective-permute-start.6 = (f32[512,256]{0,1:T(8,128)S(1)}, f32[512,256]{0,1:T(8,128)S(1)}, u32[]{:S(2)}, u32[]{:S(2)}) collective-permute-start(f32[512,256]{0,1:T(8,128)S(1)} %get-tuple-element.453), channel_id=1, source_target_pairs={{0,504},{4,508},{8,0},{12,4},{16,8},{20,12},{24,16},{28,20},{32,24... | collective-permute-start | bytes 1572872 | tf_op jit(solution)/shard_map/ppermute | solution.py:20
  928.4 17.9 %collective-permute-start.7 = (f32[512,256]{0,1:T(8,128)S(1)}, f32[512,256]{0,1:T(8,128)S(1)}, u32[]{:S(2)}, u32[]{:S(2)}) collective-permute-start(f32[512,256]{0,1:T(8,128)S(1)} %get-tuple-element.455), channel_id=1, source_target_pairs={{0,508},{4,0},{8,4},{12,8},{16,12},{20,16},{24,20},{28,24},{32,28}... | collective-permute-start | bytes 1572872 | tf_op jit(solution)/shard_map/ppermute | solution.py:20
  934.0 12.6 %collective-permute-start.8 = (f32[512,256]{0,1:T(8,128)S(1)}, f32[512,256]{0,1:T(8,128)S(1)}, u32[]{:S(2)}, u32[]{:S(2)}) collective-permute-start(f32[512,256]{0,1:T(8,128)S(1)} %get-tuple-element.454), channel_id=1, source_target_pairs={{0,4},{4,8},{8,12},{12,16},{16,20},{20,24},{24,28},{28,32},{32,36}... | collective-permute-start | bytes 1572872 | tf_op jit(solution)/shard_map/ppermute | solution.py:20
  947.7 9.8 collective-permute-start.10
  953.3 7.7 collective-permute-start.11
  955.2 6.2 collective-permute-start.9
  (7 other events, 5.2 us)
Sparse Core Ops, SparseCore 0:
  947.8 27.8 reduce-scatter.1
where the time goes:
time: 987 us; the launch traced here: 983 us
  other arithmetic  677 us (69%)
  local copies, waits for them, and re-layouts  117 us (12%)
  loops' own time  51.7 us (5%)
  matrix products  50.4 us (5%)
  starting transfers between devices  43.5 us (4%)
  waiting for transfers between devices  28.5 us (3%)
  between operations  14.4 us (1%)
    another operation x60, other arithmetic, block_loss(): factor = jnp.linalg.cholesky(kernel)  346 us
    scatter-add x8, other arithmetic, block_loss(): tail_diag = jnp.diagonal(factor)[points - PTS:]  169 us
    another operation x8, other arithmetic, block_loss(): solved = jax.scipy.linalg.solve_triangular(factor, values, lower=True)  118 us
    another operation x1, loops' own time, per_device(): lax.fori_loop(0, blocks, add_block, initial)  50.8 us
    ppermute x12, starting transfers between devices, passed_along(): return lax.ppermute(value, axis, pairs)  43.4 us
    another operation x60, local copies, waits for them, and re-layouts, block_loss(): solved = jax.scipy.linalg.solve_triangular(factor, values, lower=True)  24.6 us
    another operation x60, local copies, waits for them, and re-layouts  24.6 us
    another operation x56, matrix products, block_loss(): factor = jnp.linalg.cholesky(kernel)  24 us
  transfers between devices with their start and end apart: 13, of which 7 were waited for; matrix products, arithmetic and copies ran while one was open for 0% of the time, Pallas kernels for 0%

commit v1 on v0

v1 whole, which is shorter than its diff:
```python
import functools

import jax
import jax.numpy as jnp
from jax import lax
from jax.experimental import pallas as pl
from jax.experimental.pallas import tpu as pltpu
from jax.sharding import PartitionSpec as P

F = 256
PTS = 128
NCOND = 2
T_SIZE = 128
ORDER = PTS * (NCOND + 1)
PANEL = 8
HIGHEST = lax.Precision.HIGHEST

linear_scale = 1.0
gauss_scale = 1.5
nugget = 0.1


def mm(a, b, ca, cb, precision=HIGHEST):
    return lax.dot_general(
        a, b, (((ca,), (cb,)), ((), ())), precision=precision, preferred_element_type=jnp.float32
    )


def splat(value):
    return jnp.broadcast_to(value, (PANEL, PTS))


def inverse_factor(matrix, store):
    count = PTS // PANEL
    lane = lax.broadcasted_iota(jnp.int32, (PANEL, PTS), 1)
    sub = lax.broadcasted_iota(jnp.int32, (PANEL, PTS), 0)
    tiles = [matrix[PANEL * t : PANEL * (t + 1), :] for t in range(count)]
    for j in range(count):
        first = PANEL * j
        tile = tiles[j]
        inside = (lane >= first) & (lane < first + PANEL)
        elem = [
            [splat(tile[i : i + 1, first + k : first + k + 1]) for k in range(i + 1)]
            for i in range(PANEL)
        ]
        held = jnp.where(inside, jnp.where(lane == first + sub, 1.0, 0.0), tile)
        rows = [splat(held[i : i + 1, :]) for i in range(PANEL)]
        recip = []
        for k in range(PANEL):
            recip.append(1.0 / elem[k][k])
            pivots = [elem[m][k] for m in range(k, PANEL)]
            for i in range(k + 1, PANEL):
                scaled = elem[i][k] * recip[k]
                for m in range(k + 1, i + 1):
                    elem[i][m] = elem[i][m] - scaled * pivots[m - k]
                elem[i][k] = scaled
                rows[i] = rows[i] - scaled * rows[k]
        solved = [rows[i] * recip[i] for i in range(PANEL)]
        for k in range(PANEL - 1, 0, -1):
            for i in range(k):
                solved[i] = solved[i] - elem[k][i] * solved[k]
        whole = rows[0] * lax.rsqrt(elem[0][0])
        for i in range(1, PANEL):
            whole = jnp.where(sub == i, rows[i] * lax.rsqrt(elem[i][i]), whole)
        store(first, jnp.where(lane < first + PANEL, whole, 0.0))
        for t in range(j + 1, count):
            left = tiles[t]
            total = jnp.where(inside, 0.0, left)
            for k in range(PANEL):
                total = total - splat(left[:, first + k : first + k + 1]) * solved[k]
            tiles[t] = total


def into(ref, row, col):
    def store(first, value):
        ref[row + first : row + first + PANEL, col : col + PTS] = value

    return store


def member_places(block, cond_ref, slot_ref, blocks, total):
    listed = [cond_ref[m, block] for m in range(NCOND)] + [block]
    places = []
    for other in listed:
        slot = slot_ref[other]
        places.append((slot // blocks != block // blocks, slot % blocks))
    return places


def factor_kernel(blocks, block_ref, cond_ref, slot_ref, prev_ref, own_ref, z_ref, e_ref, la_ref, p_ref):
    block = block_ref[0]
    places = member_places(block, cond_ref, slot_ref, blocks, None)
    for m, (before, place) in enumerate(places):
        rows = pl.ds(pl.multiple_of(place * PTS, PTS), PTS)

        @pl.when(before)
        def _():
            z_ref[m * PTS : (m + 1) * PTS, :] = prev_ref[rows, :]

        @pl.when(jnp.logical_not(before))
        def _():
            z_ref[m * PTS : (m + 1) * PTS, :] = own_ref[rows, :]

    z = z_ref[...]
    gram = mm(z, z, 1, 1, None)
    eye = lax.broadcasted_iota(jnp.int32, (ORDER, ORDER), 0) == lax.broadcasted_iota(
        jnp.int32, (ORDER, ORDER), 1
    )
    diag = jnp.where(eye, gram, 0.0)
    s_row = jnp.sum(diag, axis=0, keepdims=True)
    s_col = jnp.sum(diag, axis=1, keepdims=True)
    gauss = gauss_scale * jnp.exp((s_col + s_row - 2.0 * gram) * (-1.0 / (2.0 * F)))
    e_ref[...] = gauss
    kern = gram * (linear_scale / F) + gauss + jnp.where(eye, nugget, 0.0)

    inverse_factor(kern[:PTS, :PTS], into(la_ref, 0, 0))
    x1 = la_ref[:PTS, :PTS]
    la_ref[:PTS, PTS:] = jnp.zeros((PTS, PTS), jnp.float32)
    t1 = mm(x1, kern[:PTS, PTS:], 1, 0)
    s2 = kern[PTS:, PTS:] - mm(t1, t1, 0, 0)
    inverse_factor(s2[:PTS, :PTS], into(la_ref, PTS, PTS))
    x2 = la_ref[PTS:, PTS:]
    t2 = mm(x2, s2[:PTS, PTS:], 1, 0)
    s3 = s2[PTS:, PTS:] - mm(t2, t2, 0, 0)
    r2 = -mm(x2, mm(t1[:, :PTS], x1, 0, 0), 1, 0)
    la_ref[PTS:, :PTS] = r2
    q1 = mm(t1[:, PTS:], x1, 0, 0) + mm(t2, r2, 0, 0)
    q2 = mm(t2, x2, 0, 0)
    inverse_factor(s3, into(p_ref, 0, 2 * PTS))
    x3 = p_ref[:, 2 * PTS :]
    p_ref[:, :PTS] = -mm(x3, q1, 1, 0)
    p_ref[:, PTS : 2 * PTS] = -mm(x3, q2, 1, 0)


def gradient_kernel(
    blocks, block_ref, cond_ref, slot_ref, prev_ref, own_ref, z_ref, e_ref, la_ref, p_ref, out_ref, y_ref
):
    block = block_ref[0]
    places = member_places(block, cond_ref, slot_ref, blocks, None)
    for m, (before, place) in enumerate(places):
        cols = pl.ds(pl.multiple_of(place * PTS, PTS), PTS)

        @pl.when(before)
        def _():
            y_ref[:, m * PTS : (m + 1) * PTS] = prev_ref[:, cols].astype(jnp.float32)

        @pl.when(jnp.logical_not(before))
        def _():
            y_ref[:, m * PTS : (m + 1) * PTS] = own_ref[:, cols].astype(jnp.float32)

    y = y_ref[...]
    proj = p_ref[...]
    la = la_ref[...]
    white = mm(y, proj, 1, 1)
    delta = mm(white, proj, 1, 0)
    alpha = mm(mm(y[:, : 2 * PTS], la, 1, 1), la, 1, 0)
    half = 0.5 * delta
    beta = jnp.concatenate([half[:, : 2 * PTS] + alpha, half[:, 2 * PTS :]], axis=1)
    left = jnp.concatenate([proj, delta, beta], axis=0)
    right = jnp.concatenate([(0.5 * T_SIZE) * proj, -0.5 * beta, -half], axis=0)
    grad_kern = mm(left, right, 0, 0)
    through = grad_kern * e_ref[...]
    eye = lax.broadcasted_iota(jnp.int32, (ORDER, ORDER), 0) == lax.broadcasted_iota(
        jnp.int32, (ORDER, ORDER), 1
    )
    summed = jnp.sum(through, axis=1, keepdims=True)
    both = (linear_scale * grad_kern + through - jnp.where(eye, summed, 0.0)) * (2.0 / F)
    high = both.astype(jnp.bfloat16)
    low = (both - high.astype(jnp.float32)).astype(jnp.bfloat16)
    z = z_ref[...]
    grad_z = mm(z, high, 0, 0, None) + mm(z, low, 0, 0, None)
    parts = out_ref.shape[0]
    zw = F // parts
    tw = T_SIZE // parts
    for part in range(parts):
        for place, m in enumerate((NCOND,) + tuple(range(NCOND))):
            cols = slice(m * PTS, (m + 1) * PTS)
            row = 0 if place == 0 else zw + 2 * tw + (place - 1) * (zw + tw)
            out_ref[part, row : row + zw, :] = grad_z[part * zw : (part + 1) * zw, cols]
            out_ref[part, row + zw : row + zw + tw, :] = delta[part * tw : (part + 1) * tw, cols]
        out_ref[part, zw + tw : zw + 2 * tw, :] = white[part * tw : (part + 1) * tw, :]


def combine_kernel(blocks, zw, tw, block_ref, cond_ref, slot_ref, got_ref, white_ref, own_ref, prev_ref):
    parts = got_ref.shape[0]
    height = zw + tw
    base = block_ref[0] // blocks * blocks
    own_ref[...] = jnp.zeros_like(own_ref)
    prev_ref[...] = jnp.zeros_like(prev_ref)
    for source in range(parts):
        places = member_places(base + source, cond_ref, slot_ref, blocks, None)
        for m, (before, place) in enumerate(places):
            cols = pl.ds(pl.multiple_of(place * PTS, PTS), PTS)
            row = 0 if m == NCOND else height + tw + m * height
            value = got_ref[source, row : row + height, :]
            if m == NCOND:
                own_ref[:, cols] += value
                white_ref[:, cols] = got_ref[source, height : height + tw, :]
            else:

                @pl.when(before)
                def _():
                    prev_ref[:, cols] += value

                @pl.when(jnp.logical_not(before))
                def _():
                    own_ref[:, cols] += value


def passed_along(value, axis, steps):
    count = lax.axis_size(axis)
    pairs = [(source, (source + steps) % count) for source in range(count)]
    return lax.ppermute(value, axis, pairs)


VMEM = pl.BlockSpec(memory_space=pltpu.VMEM)
SMEM = pl.BlockSpec(memory_space=pltpu.SMEM)


def shape(*dims, dtype=jnp.float32):
    return jax.ShapeDtypeStruct(dims, dtype)


def factor_call(blocks, block, cond, slots, prev, own):
    return pl.pallas_call(
        functools.partial(factor_kernel, blocks),
        out_shape=(
            shape(ORDER, F, dtype=jnp.bfloat16),
            shape(ORDER, ORDER),
            shape(2 * PTS, 2 * PTS),
            shape(PTS, ORDER),
        ),
        in_specs=[SMEM] * 3 + [VMEM] * 2,
        out_specs=(VMEM,) * 4,
        name="factor",
    )(block, cond, slots, prev, own)


def gradient_call(blocks, parts, block, cond, slots, prev, own, z, e, la, p):
    height = 3 * (F + T_SIZE) // parts + T_SIZE // parts
    return pl.pallas_call(
        functools.partial(gradient_kernel, blocks),
        out_shape=shape(parts, height, PTS),
        in_specs=[SMEM] * 3 + [VMEM] * 6,
        out_specs=VMEM,
        scratch_shapes=[pltpu.VMEM((T_SIZE, ORDER), jnp.float32)],
        name="gradient",
    )(block, cond, slots, prev, own, z, e, la, p)


def combine_call(blocks, parts, block, cond, slots, got):
    zw, tw = F // parts, T_SIZE // parts
    rows = blocks * PTS
    return pl.pallas_call(
        functools.partial(combine_kernel, blocks, zw, tw),
        out_shape=(shape(tw, rows), shape(zw + tw, rows), shape(zw + tw, rows)),
        in_specs=[SMEM] * 3 + [VMEM],
        out_specs=(VMEM,) * 3,
        name="combine",
    )(block, cond, slots, got)


def per_device(features, targets, conditioning, block_slot):
    parts = lax.axis_size("rep")
    blocks = features.shape[0] // PTS
    block = (lax.axis_index("blk") * blocks + lax.axis_index("rep")).astype(jnp.int32)[None]
    cond = conditioning.T
    prev_features = passed_along(features, "blk", 1)
    columns = targets.T
    gathered = lax.all_to_all(
        jnp.broadcast_to(columns[None], (parts,) + columns.shape), "rep", 0, 0, tiled=True
    ).reshape(T_SIZE, features.shape[0])
    prev_targets = passed_along(gathered, "blk", 1)
    z, e, la, p = factor_call(blocks, block, cond, block_slot, prev_features, features)
    sent = gradient_call(
        blocks, parts, block, cond, block_slot, prev_targets, gathered, z, e, la, p
    )
    got = lax.all_to_all(sent, "rep", 0, 0, tiled=True)
    white, own, prev = combine_call(blocks, parts, block, cond, block_slot, got)
    own = own + passed_along(prev, "blk", -1)
    zw = F // parts
    return (white.T, own[:zw].T, own[zw:].T)


def solution(mesh):
    in_specs = (P("blk", None), P("blk", "rep"), P(), P())
    out_specs = (P("blk", "rep"), P("blk", "rep"), P("blk", "rep"))
    return jax.shard_map(
        per_device, mesh=mesh, in_specs=in_specs, out_specs=out_specs, check_vma=False
    )
```

time: 987 us -> 75 us (0.08)
  the two profiles are of different devices: /device:TPU:16 before, /device:TPU:2 now
where the time goes in v1:
time: 75 us; the launch traced here: 74.6 us
  Pallas kernels  28.4 us (38%)
  blocking collectives  27 us (36%)
  starting transfers between devices  10.5 us (14%)
  waiting for transfers between devices  3.63 us (5%)
  local copies, waits for them, and re-layouts  3.42 us (5%)
  other arithmetic  0.96 us (1%)
    pallas_call x1, Pallas kernels, factor_call(): pl.pallas_call(functools.partial(factor_kernel, blocks), out_shape=(shape...  20.7 us
    all_to_all x1, blocking collectives, per_device(): got = lax.all_to_all(sent, 'rep', 0, 0, tiled=True)  14.3 us
    all_to_all x1, blocking collectives, per_device(): lax.all_to_all(jnp.broadcast_to(columns[None], (parts,) + columns.shape),...  12.8 us
    ppermute x3, starting transfers between devices, passed_along(): return lax.ppermute(value, axis, pairs)  10.5 us
    pallas_call x1, Pallas kernels, gradient_call(): pl.pallas_call(functools.partial(gradient_kernel, blocks), out_shape=shap...  5.62 us
    ppermute x3, waiting for transfers between devices, passed_along(): return lax.ppermute(value, axis, pairs)  3.63 us
    pallas_call x1, Pallas kernels, combine_call(): pl.pallas_call(functools.partial(combine_kernel, blocks, zw, tw), out_sha...  2.08 us
  transfers between devices with their start and end apart: 3, of which 2 were waited for; matrix products, arithmetic and copies ran while one was open for 1% of the time, Pallas kernels for 28%

profile of v1, /device:TPU:2, one launch (start us, length us, event | category | flops | bytes accessed | tf_op | source)
XLA Modules:
  0.0 74.6 jit_solution(275152283433786268)
XLA Ops:
  0.6 1.9 %collective-permute-start.1 = (bf16[512,256]{1,0:T(8,128)(2,1)}, bf16[512,256]{1,0:T(8,128)(2,1)S(1)}, u32[]{:S(2)}, u32[]{:S(2)}) collective-permute-start(bf16[512,256]{1,0:T(8,128)(2,1)} %own_ref.1), channel_id=1, source_target_pairs={{0,4},{4,8},{8,12},{12,16},{16,20},{20,24},{24,28},{28,32},{32,36}... | collective-permute-start | bytes 786440 | tf_op jit(solution)/shard_map/ppermute | solution.py:213
  2.6 0.8 %broadcast_in_dim.10 = bf16[4,32,512]{2,1,0:T(8,128)(2,1)S(1)} broadcast(bf16[32,512]{1,0:T(8,128)(2,1)} %bitcast.14), dimensions={1,2} | broadcast | bytes 163840 | tf_op jit(solution)/shard_map/broadcast_in_dim | solution.py:271
  3.3 12.8 %all_to_all.10 = bf16[4,32,512]{2,1,0:T(8,128)(2,1)S(1)} all-to-all(bf16[4,32,512]{2,1,0:T(8,128)(2,1)S(1)} %broadcast_in_dim.10), channel_id=1, replica_groups=mesh['blk'=128,'rep'=4] {'rep'}, dimensions={0} | all-to-all | bytes 262144 | tf_op jit(solution)/shard_map/all_to_all | solution.py:270
  16.1 0.0 copy-start
  16.1 1.9 %collective-permute-start = (bf16[128,512]{1,0:T(8,128)(2,1)S(1)}, bf16[128,512]{1,0:T(8,128)(2,1)S(1)}, u32[]{:S(2)}, u32[]{:S(2)}) collective-permute-start(bf16[128,512]{1,0:T(8,128)(2,1)S(1)} %bitcast.9), channel_id=1, source_target_pairs={{0,4},{4,8},{8,12},{12,16},{16,20},{20,24},{24,28},{28,32},{32,36}... | collective-permute-start | bytes 393224 | tf_op jit(solution)/shard_map/ppermute | solution.py:213
  18.0 0.1 collective-permute-done.1.prev_ref
  18.2 0.0 copy-start.1
  18.2 0.7 copy-done.1
  18.9 20.7 %factor.1 = (bf16[384,256]{1,0:T(8,128)(2,1)}, f32[384,384]{1,0:T(8,128)}, f32[256,256]{1,0:T(8,128)}, f32[128,384]{1,0:T(8,128)}) custom-call(s32[1]{0:T(128)} %bitcast.block_ref, s32[2,512]{1,0:T(2,128)} %bitcast.11, s32[512]{0:T(512)} %slot_ref.5, bf16[512,256]{1,0:T(8,128)(2,1)} %copy-done.1, bf16[512,256]{1,0:T(8,128)(2,1)} %own_ref.1), custom_call_target="tpu_custom_call" | custom-call | tf_op jit(solution)/shard_map/factor/pallas_call | solution.py:225
  39.6 0.0 copy-done
  39.6 0.0 collective-permute-done.prev_ref
  39.6 0.0 copy-start.2
  39.6 0.6 copy-done.2
  40.2 5.6 %gradient.1 = f32[4,320,128]{2,1,0:T(8,128)} custom-call(s32[1]{0:T(128)} %bitcast.block_ref, s32[2,512]{1,0:T(2,128)} %bitcast.12, s32[512]{0:T(512)} %slot_ref.5, bf16[128,512]{1,0:T(8,128)(2,1)} %copy-done.2, bf16[128,512]{1,0:T(8,128)(2,1)} %bitcast.10, bf16[384,256]{1,0:T(8,128)(2,1)} %get-tuple-element.10.z_ref, f32[384,384]{1,0:T(8,128)} %get-tuple-element.11.e_ref, ...), custom_call_target="tpu_custom_call" | custom-call | tf_op jit(solution)/shard_map/gradient/pallas_call | solution.py:241
  45.8 14.3 %all_to_all.11.got_ref = f32[4,320,128]{2,1,0:T(8,128)} all-to-all(f32[4,320,128]{2,1,0:T(8,128)} %gradient.1), channel_id=1, replica_groups=mesh['blk'=128,'rep'=4] {'rep'}, dimensions={0} | all-to-all | bytes 1310720 | tf_op jit(solution)/shard_map/all_to_all | solution.py:278
  60.1 2.1 %combine.1 = (f32[32,512]{1,0:T(8,128)}, f32[96,512]{1,0:T(8,128)}, f32[96,512]{1,0:T(8,128)}) custom-call(s32[1]{0:T(128)} %bitcast.block_ref, s32[2,512]{1,0:T(2,128)} %bitcast.13, s32[512]{0:T(512)} %slot_ref.5, f32[4,320,128]{2,1,0:T(8,128)} %all_to_all.11.got_ref), custom_call_target="tpu_custom_call" | custom-call | tf_op jit(solution)/shard_map/combine/pallas_call | solution.py:254
  62.2 6.6 %collective-permute-start.2 = (f32[96,512]{1,0:T(8,128)}, f32[96,512]{1,0:T(8,128)S(1)}, u32[]{:S(2)}, u32[]{:S(2)}) collective-permute-start(f32[96,512]{1,0:T(8,128)} %get-tuple-element.16), channel_id=1, source_target_pairs={{0,508},{4,0},{8,4},{12,8},{16,12},{20,16},{24,20},{28,24},{32,28}... | collective-permute-start | bytes 589832 | tf_op jit(solution)/shard_map/ppermute | solution.py:213
  68.8 3.5 %collective-permute-done.2 = f32[96,512]{1,0:T(8,128)S(1)} collective-permute-done((f32[96,512]{1,0:T(8,128)}, f32[96,512]{1,0:T(8,128)S(1)}, u32[]{:S(2)}, u32[]{:S(2)}) %collective-permute-start.2) | collective-permute-done | bytes 196640 | tf_op jit(solution)/shard_map/ppermute | solution.py:213
  72.3 1.0 %add.7 = f32[96,512]{1,0:T(8,128)S(1)} add(f32[96,512]{1,0:T(8,128)} %get-tuple-element.15, f32[96,512]{1,0:T(8,128)S(1)} %collective-permute-done.2) | non-fusion elementwise | flops 49152 | bytes 589824 | tf_op jit(solution)/shard_map/add | solution.py:280
  73.3 0.6 slice_bitcast_fusion.1
  73.9 0.7 slice_bitcast_fusion
Async XLA Ops:
  0.6 17.6 %collective-permute-start.1 = (bf16[512,256]{1,0:T(8,128)(2,1)}, bf16[512,256]{1,0:T(8,128)(2,1)S(1)}, u32[]{:S(2)}, u32[]{:S(2)}) collective-permute-start(bf16[512,256]{1,0:T(8,128)(2,1)} %own_ref.1), channel_id=1, source_target_pairs={{0,4},{4,8},{8,12},{12,16},{16,20},{20,24},{24,28},{28,32},{32,36}... | collective-permute-start | bytes 786440 | tf_op jit(solution)/shard_map/ppermute | solution.py:213
  16.1 23.4 %copy-start = (bf16[4,32,512]{2,1,0:T(8,128)(2,1)}, bf16[4,32,512]{2,1,0:T(8,128)(2,1)S(1)}, u32[]{:S(2)}) copy-start(bf16[4,32,512]{2,1,0:T(8,128)(2,1)S(1)} %all_to_all.10) | copy-start | bytes 393220
  16.1 23.4 %collective-permute-start = (bf16[128,512]{1,0:T(8,128)(2,1)S(1)}, bf16[128,512]{1,0:T(8,128)(2,1)S(1)}, u32[]{:S(2)}, u32[]{:S(2)}) collective-permute-start(bf16[128,512]{1,0:T(8,128)(2,1)S(1)} %bitcast.9), channel_id=1, source_target_pairs={{0,4},{4,8},{8,12},{12,16},{16,20},{20,24},{24,28},{28,32},{32,36}... | collective-permute-start | bytes 393224 | tf_op jit(solution)/shard_map/ppermute | solution.py:213
  18.2 0.7 copy-start.1
  39.6 0.7 copy-start.2
  62.2 10.1 %collective-permute-start.2 = (f32[96,512]{1,0:T(8,128)}, f32[96,512]{1,0:T(8,128)S(1)}, u32[]{:S(2)}, u32[]{:S(2)}) collective-permute-start(f32[96,512]{1,0:T(8,128)} %get-tuple-element.16), channel_id=1, source_target_pairs={{0,508},{4,0},{8,4},{12,8},{16,12},{20,16},{24,20},{28,24},{32,28}... | collective-permute-start | bytes 589832 | tf_op jit(solution)/shard_map/ppermute | solution.py:213

commit v2 on v1

--- a/solution.py
+++ b/solution.py
@@ -26,8 +26,26 @@
     )
 
 
+def halves(value):
+    high = value.astype(jnp.bfloat16)
+    return high, (value - high.astype(jnp.float32)).astype(jnp.bfloat16)
+
+
+def mm3(a, b, ca, cb):
+    (ah, al), (bh, bl) = halves(a), halves(b)
+    return mm(ah, bl, ca, cb, None) + mm(al, bh, ca, cb, None) + mm(ah, bh, ca, cb, None)
+
+
 def splat(value):
     return jnp.broadcast_to(value, (PANEL, PTS))
+
+
+def across(tile, lane):
+    return splat(tile[:, lane : lane + 1])
+
+
+def down(tile, row):
+    return splat(tile[row : row + 1, :])
 
 
 def inverse_factor(matrix, store):
@@ -35,40 +53,53 @@
     lane = lax.broadcasted_iota(jnp.int32, (PANEL, PTS), 1)
     sub = lax.broadcasted_iota(jnp.int32, (PANEL, PTS), 0)
     tiles = [matrix[PANEL * t : PANEL * (t + 1), :] for t in range(count)]
+    cols = [across(tiles[0], m) for m in range(PANEL)]
     for j in range(count):
         first = PANEL * j
-        tile = tiles[j]
+        more = j + 1 < count
         inside = (lane >= first) & (lane < first + PANEL)
-        elem = [
-            [splat(tile[i : i + 1, first + k : first + k + 1]) for k in range(i + 1)]
-            for i in range(PANEL)
-        ]
-        held = jnp.where(inside, jnp.where(lane == first + sub, 1.0, 0.0), tile)
-        rows = [splat(held[i : i + 1, :]) for i in range(PANEL)]
-        recip = []
+        held = jnp.where(inside, jnp.where(lane == first + sub, 1.0, 0.0), tiles[j])
+        if more:
+            coef = [across(tiles[j + 1], first + m) for m in range(PANEL)]
+            ahead = [across(tiles[j + 1], first + PANEL + m) for m in range(PANEL)]
+            after = jnp.where(inside, 0.0, tiles[j + 1])
+        recip, lower, rows = [], [], []
+        scale = None
         for k in range(PANEL):
-            recip.append(1.0 / elem[k][k])
-            pivots = [elem[m][k] for m in range(k, PANEL)]
-            for i in range(k + 1, PANEL):
-                scaled = elem[i][k] * recip[k]
-                for m in range(k + 1, i + 1):
-                    elem[i][m] = elem[i][m] - scaled * pivots[m - k]
-                elem[i][k] = scaled
-                rows[i] = rows[i] - scaled * rows[k]
-        solved = [rows[i] * recip[i] for i in range(PANEL)]
-        for k in range(PANEL - 1, 0, -1):
-            for i in range(k):
-                solved[i] = solved[i] - elem[k][i] * solved[k]
-        whole = rows[0] * lax.rsqrt(elem[0][0])
-        for i in range(1, PANEL):
-            whole = jnp.where(sub == i, rows[i] * lax.rsqrt(elem[i][i]), whole)
-        store(first, jnp.where(lane < first + PANEL, whole, 0.0))
-        for t in range(j + 1, count):
-            left = tiles[t]
-            total = jnp.where(inside, 0.0, left)
+            pivot = down(cols[k], k)
+            recip.append(1.0 / pivot)
+            root = lax.rsqrt(pivot)
+            scale = root if scale is None else jnp.where(sub == k, root, scale)
+            below = {m: down(cols[k], m) for m in range(k + 1, PANEL)}
+            lower.append({m: below[m] * recip[k] for m in below})
+            rows.append(down(held, k))
+            if below:
+                factor = jnp.where(sub > k, cols[k] * recip[k], 0.0)
+                for m in below:
+                    cols[m] = cols[m] - factor * below[m]
+                held = held - factor * rows[k]
+            if more:
+                factor = coef[k] * recip[k]
+                for m in range(PANEL):
+                    ahead[m] = ahead[m] - factor * down(coef[k], m)
+                for m in below:
+                    coef[m] = coef[m] - factor * below[m]
+                after = after - factor * rows[k]
+        store(first, jnp.where(lane < first + PANEL, held * scale, 0.0))
+        if not more:
+            break
+        if j + 2 < count:
+            solved = [rows[i] * recip[i] for i in range(PANEL)]
+            for k in range(PANEL - 1, 0, -1):
+                for i in range(k):
+                    solved[i] = solved[i] - lower[i][k] * solved[k]
+        for t in range(j + 2, count):
+            total = jnp.where(inside, 0.0, tiles[t])
             for k in range(PANEL):
-                total = total - splat(left[:, first + k : first + k + 1]) * solved[k]
+                total = total - across(tiles[t], first + k) * solved[k]
             tiles[t] = total
+        tiles[j + 1] = after
+        cols = ahead
 
 
 def into(ref, row, col):
@@ -87,20 +118,31 @@
     return places
 
 
-def factor_kernel(blocks, block_ref, cond_ref, slot_ref, prev_ref, own_ref, z_ref, e_ref, la_ref, p_ref):
+def fetch(places, prev_ref, own_ref, into_ref, sems, dim):
+    def window(ref, start):
+        span = pl.ds(pl.multiple_of(start * PTS, PTS), PTS)
+        return ref.at[span, :] if dim == 0 else ref.at[:, span]
+
+    for m, (before, place) in enumerate(places):
+
+        @pl.when(before)
+        def _():
+            pltpu.make_async_copy(window(prev_ref, place), window(into_ref, m), sems.at[m]).start()
+
+        @pl.when(jnp.logical_not(before))
+        def _():
+            pltpu.make_async_copy(window(own_ref, place), window(into_ref, m), sems.at[m]).start()
+
+    for m, (before, place) in enumerate(places):
+        pltpu.make_async_copy(window(own_ref, place), window(into_ref, m), sems.at[m]).wait()
+
+
+def factor_kernel(
+    blocks, block_ref, cond_ref, slot_ref, prev_ref, own_ref, z_ref, e_ref, la_ref, p_ref, sems
+):
     block = block_ref[0]
     places = member_places(block, cond_ref, slot_ref, blocks, None)
-    for m, (before, place) in enumerate(places):
-        rows = pl.ds(pl.multiple_of(place * PTS, PTS), PTS)
-
-        @pl.when(before)
-        def _():
-            z_ref[m * PTS : (m + 1) * PTS, :] = prev_ref[rows, :]
-
-        @pl.when(jnp.logical_not(before))
-        def _():
-            z_ref[m * PTS : (m + 1) * PTS, :] = own_ref[rows, :]
-
+    fetch(places, prev_ref, own_ref, z_ref, sems, 0)
     z = z_ref[...]
     gram = mm(z, z, 1, 1, None)
     eye = lax.broadcasted_iota(jnp.int32, (ORDER, ORDER), 0) == lax.broadcasted_iota(
@@ -116,15 +158,21 @@
     inverse_factor(kern[:PTS, :PTS], into(la_ref, 0, 0))
     x1 = la_ref[:PTS, :PTS]
     la_ref[:PTS, PTS:] = jnp.zeros((PTS, PTS), jnp.float32)
-    t1 = mm(x1, kern[:PTS, PTS:], 1, 0)
-    s2 = kern[PTS:, PTS:] - mm(t1, t1, 0, 0)
-    inverse_factor(s2[:PTS, :PTS], into(la_ref, PTS, PTS))
+    k12, k13 = kern[:PTS, PTS : 2 * PTS], kern[:PTS, 2 * PTS :]
+    t12 = mm(x1, k12, 1, 0)
+    s22 = kern[PTS : 2 * PTS, PTS : 2 * PTS] - mm(t12, t12, 0, 0)
+    inverse_factor(s22, into(la_ref, PTS, PTS))
     x2 = la_ref[PTS:, PTS:]
-    t2 = mm(x2, s2[:PTS, PTS:], 1, 0)
-    s3 = s2[PTS:, PTS:] - mm(t2, t2, 0, 0)
-    r2 = -mm(x2, mm(t1[:, :PTS], x1, 0, 0), 1, 0)
+    t13 = mm(x1, k13, 1, 0)
+    s23 = kern[PTS : 2 * PTS, 2 * PTS :] - mm(t12, t13, 0, 0)
+    s33 = kern[2 * PTS :, 2 * PTS :] - mm(t13, t13, 0, 0)
+    u12 = mm(t12, x1, 0, 0)
+    u13 = mm(t13, x1, 0, 0)
+    t2 = mm(x2, s23, 1, 0)
+    s3 = s33 - mm(t2, t2, 0, 0)
+    r2 = -mm(x2, u12, 1, 0)
     la_ref[PTS:, :PTS] = r2
-    q1 = mm(t1[:, PTS:], x1, 0, 0) + mm(t2, r2, 0, 0)
+    q1 = u13 + mm(t2, r2, 0, 0)
     q2 = mm(t2, x2, 0, 0)
     inverse_factor(s3, into(p_ref, 0, 2 * PTS))
     x3 = p_ref[:, 2 * PTS :]
@@ -133,40 +181,29 @@
 
 
 def gradient_kernel(
-    blocks, block_ref, cond_ref, slot_ref, prev_ref, own_ref, z_ref, e_ref, la_ref, p_ref, out_ref, y_ref
+    blocks, block_ref, cond_ref, slot_ref, prev_ref, own_ref, z_ref, e_ref, la_ref, p_ref, out_ref, y_ref, sems
 ):
     block = block_ref[0]
     places = member_places(block, cond_ref, slot_ref, blocks, None)
-    for m, (before, place) in enumerate(places):
-        cols = pl.ds(pl.multiple_of(place * PTS, PTS), PTS)
-
-        @pl.when(before)
-        def _():
-            y_ref[:, m * PTS : (m + 1) * PTS] = prev_ref[:, cols].astype(jnp.float32)
-
-        @pl.when(jnp.logical_not(before))
-        def _():
-            y_ref[:, m * PTS : (m + 1) * PTS] = own_ref[:, cols].astype(jnp.float32)
-
-    y = y_ref[...]
+    fetch(places, prev_ref, own_ref, y_ref, sems, 1)
+    y = y_ref[...].astype(jnp.float32)
     proj = p_ref[...]
     la = la_ref[...]
-    white = mm(y, proj, 1, 1)
-    delta = mm(white, proj, 1, 0)
-    alpha = mm(mm(y[:, : 2 * PTS], la, 1, 1), la, 1, 0)
+    white = mm3(y, proj, 1, 1)
+    delta = mm3(white, proj, 1, 0)
+    alpha = mm3(mm3(y[:, : 2 * PTS], la, 1, 1), la, 1, 0)
     half = 0.5 * delta
     beta = jnp.concatenate([half[:, : 2 * PTS] + alpha, half[:, 2 * PTS :]], axis=1)
     left = jnp.concatenate([proj, delta, beta], axis=0)
     right = jnp.concatenate([(0.5 * T_SIZE) * proj, -0.5 * beta, -half], axis=0)
-    grad_kern = mm(left, right, 0, 0)
+    grad_kern = mm3(left, right, 0, 0)
     through = grad_kern * e_ref[...]
     eye = lax.broadcasted_iota(jnp.int32, (ORDER, ORDER), 0) == lax.broadcasted_iota(
         jnp.int32, (ORDER, ORDER), 1
     )
     summed = jnp.sum(through, axis=1, keepdims=True)
     both = (linear_scale * grad_kern + through - jnp.where(eye, summed, 0.0)) * (2.0 / F)
-    high = both.astype(jnp.bfloat16)
-    low = (both - high.astype(jnp.float32)).astype(jnp.bfloat16)
+    high, low = halves(both)
     z = z_ref[...]
     grad_z = mm(z, high, 0, 0, None) + mm(z, low, 0, 0, None)
     parts = out_ref.shape[0]
@@ -215,6 +252,7 @@
 
 VMEM = pl.BlockSpec(memory_space=pltpu.VMEM)
 SMEM = pl.BlockSpec(memory_space=pltpu.SMEM)
+ANY = pl.BlockSpec(memory_space=pl.ANY)
 
 
 def shape(*dims, dtype=jnp.float32):
@@ -230,8 +268,9 @@
             shape(2 * PTS, 2 * PTS),
             shape(PTS, ORDER),
         ),
-        in_specs=[SMEM] * 3 + [VMEM] * 2,
+        in_specs=[SMEM] * 3 + [ANY] * 2,
         out_specs=(VMEM,) * 4,
+        scratch_shapes=[pltpu.SemaphoreType.DMA((NCOND + 1,))],
         name="factor",
     )(block, cond, slots, prev, own)
 
@@ -241,9 +280,12 @@
     return pl.pallas_call(
         functools.partial(gradient_kernel, blocks),
         out_shape=shape(parts, height, PTS),
-        in_specs=[SMEM] * 3 + [VMEM] * 6,
+        in_specs=[SMEM] * 3 + [ANY] * 2 + [VMEM] * 4,
         out_specs=VMEM,
-        scratch_shapes=[pltpu.VMEM((T_SIZE, ORDER), jnp.float32)],
+        scratch_shapes=[
+            pltpu.VMEM((T_SIZE, ORDER), jnp.bfloat16),
+            pltpu.SemaphoreType.DMA((NCOND + 1,)),
+        ],
         name="gradient",
     )(block, cond, slots, prev, own, z, e, la, p)
 
@@ -258,6 +300,23 @@
         out_specs=(VMEM,) * 3,
         name="combine",
     )(block, cond, slots, got)
+
+
+def sum_kernel(own_ref, more_ref, z_ref, y_ref):
+    zw = z_ref.shape[0]
+    z_ref[...] = own_ref[:zw, :] + more_ref[:zw, :]
+    y_ref[...] = own_ref[zw:, :] + more_ref[zw:, :]
+
+
+def sum_call(parts, own, more):
+    rows = own.shape[1]
+    return pl.pallas_call(
+        sum_kernel,
+        out_shape=(shape(F // parts, rows), shape(T_SIZE // parts, rows)),
+        in_specs=[VMEM] * 2,
+        out_specs=(VMEM,) * 2,
+        name="total",
+    )(own, more)
 
 
 def per_device(features, targets, conditioning, block_slot):
@@ -277,9 +336,8 @@
     )
     got = lax.all_to_all(sent, "rep", 0, 0, tiled=True)
     white, own, prev = combine_call(blocks, parts, block, cond, block_slot, got)
-    own = own + passed_along(prev, "blk", -1)
-    zw = F // parts
-    return (white.T, own[:zw].T, own[zw:].T)
+    grad_z, grad_y = sum_call(parts, own, passed_along(prev, "blk", -1))
+    return (white.T, grad_z.T, grad_y.T)
 
 
 def solution(mesh):

time: 75 us -> 66.6 us (0.89)
  Pallas kernels: 28.4 us -> 21.4 us
  other arithmetic: 0.96 us -> 0 us
    pallas_call x1, Pallas kernels: 20.7 us -> 12.6 us  [factor_call(): pl.pallas_call(functools.partial(factor_kernel, blocks), out_shape=(shape...]
    pallas_call x0 -> x1, Pallas kernels: none -> 1.71 us  [sum_call(): pl.pallas_call(sum_kernel, out_shape=(shape(F // parts, rows), shape(T_SI...]
    transpose x2 -> x0, local copies, waits for them, and re-layouts: 1.3 us -> none  [per_device(): return (white.T, own[:zw].T, own[zw:].T)]
    add x1 -> x0, other arithmetic: 0.96 us -> none  [per_device(): own = own + passed_along(prev, 'blk', -1)]
    unnamed x6 -> x8, local copies, waits for them, and re-layouts: 1.35 us -> 2.01 us
  transfers between devices with their start and end apart: 3 -> 3, of which waited for: 2 -> 2; matrix products, arithmetic and copies ran while one was open for 1% -> 1% of each run, Pallas kernels for 28% -> 19%
where the time goes in v2:
time: 66.6 us; the launch traced here: 66.1 us
  blocking collectives  27.1 us (41%)
  Pallas kernels  21.4 us (32%)
  starting transfers between devices  10.5 us (16%)
  waiting for transfers between devices  3.63 us (5%)
  local copies, waits for them, and re-layouts  2.78 us (4%)
  between operations  0.71 us (1%)
    all_to_all x1, blocking collectives, per_device(): got = lax.all_to_all(sent, 'rep', 0, 0, tiled=True)  14.3 us
    all_to_all x1, blocking collectives, per_device(): lax.all_to_all(jnp.broadcast_to(columns[None], (parts,) + columns.shape),...  12.8 us
    pallas_call x1, Pallas kernels, factor_call(): pl.pallas_call(functools.partial(factor_kernel, blocks), out_shape=(shape...  12.6 us
    ppermute x3, starting transfers between devices, passed_along(): return lax.ppermute(value, axis, pairs)  10.5 us
    pallas_call x1, Pallas kernels, gradient_call(): pl.pallas_call(functools.partial(gradient_kernel, blocks), out_shape=shap...  5 us
    ppermute x3, waiting for transfers between devices, passed_along(): return lax.ppermute(value, axis, pairs)  3.63 us
    pallas_call x1, Pallas kernels, combine_call(): pl.pallas_call(functools.partial(combine_kernel, blocks, zw, tw), out_sha...  2.07 us
    unnamed x8, local copies, waits for them, and re-layouts  2.01 us
  transfers between devices with their start and end apart: 3, of which 2 were waited for; matrix products, arithmetic and copies ran while one was open for 1% of the time, Pallas kernels for 19%

profile of v2, /device:TPU:2, one launch (start us, length us, event | category | flops | bytes accessed | tf_op | source)
XLA Modules:
  0.0 66.1 jit_solution(798174375049284823)
XLA Ops:
  0.6 1.9 %collective-permute-start.1 = (bf16[512,256]{1,0:T(8,128)(2,1)}, bf16[512,256]{1,0:T(8,128)(2,1)S(1)}, u32[]{:S(2)}, u32[]{:S(2)}) collective-permute-start(bf16[512,256]{1,0:T(8,128)(2,1)} %own_ref.1), channel_id=1, source_target_pairs={{0,4},{4,8},{8,12},{12,16},{16,20},{20,24},{24,28},{28,32},{32,36}... | collective-permute-start | bytes 786440 | tf_op jit(solution)/shard_map/ppermute | solution.py:250
  2.6 0.8 %broadcast_in_dim.10 = bf16[4,32,512]{2,1,0:T(8,128)(2,1)S(1)} broadcast(bf16[32,512]{1,0:T(8,128)(2,1)} %bitcast.12), dimensions={1,2} | broadcast | bytes 163840 | tf_op jit(solution)/shard_map/broadcast_in_dim | solution.py:330
  3.3 12.8 %all_to_all.10 = bf16[4,32,512]{2,1,0:T(8,128)(2,1)S(1)} all-to-all(bf16[4,32,512]{2,1,0:T(8,128)(2,1)S(1)} %broadcast_in_dim.10), channel_id=1, replica_groups=mesh['blk'=128,'rep'=4] {'rep'}, dimensions={0} | all-to-all | bytes 262144 | tf_op jit(solution)/shard_map/all_to_all | solution.py:329
  16.1 0.0 copy-start
  16.1 1.9 %collective-permute-start = (bf16[128,512]{1,0:T(8,128)(2,1)S(1)}, bf16[128,512]{1,0:T(8,128)(2,1)S(1)}, u32[]{:S(2)}, u32[]{:S(2)}) collective-permute-start(bf16[128,512]{1,0:T(8,128)(2,1)S(1)} %bitcast.7), channel_id=1, source_target_pairs={{0,4},{4,8},{8,12},{12,16},{16,20},{20,24},{24,28},{28,32},{32,36}... | collective-permute-start | bytes 393224 | tf_op jit(solution)/shard_map/ppermute | solution.py:250
  18.0 0.1 collective-permute-done.1.prev_ref
  18.2 0.0 copy-start.1
  18.2 0.7 %copy-done.1 = bf16[512,256]{1,0:T(8,128)(2,1)} copy-done((bf16[512,256]{1,0:T(8,128)(2,1)}, bf16[512,256]{1,0:T(8,128)(2,1)S(1)}, u32[]{:S(2)}) %copy-start.1) | copy-done | bytes 262168
  18.9 12.6 %factor.1 = (bf16[384,256]{1,0:T(8,128)(2,1)}, f32[384,384]{1,0:T(8,128)}, f32[256,256]{1,0:T(8,128)}, f32[128,384]{1,0:T(8,128)}) custom-call(s32[1]{0:T(128)} %bitcast.block_ref, s32[2,512]{1,0:T(2,128)} %bitcast.9, s32[512]{0:T(512)} %slot_ref.5, bf16[512,256]{1,0:T(8,128)(2,1)} %copy-done.1, bf16[512,256]{1,0:T(8,128)(2,1)} %own_ref.1), custom_call_target="tpu_custom_call" | custom-call | tf_op jit(solution)/shard_map/factor/pallas_call | solution.py:263
  31.5 0.0 copy-done
  31.5 0.0 collective-permute-done.prev_ref
  31.6 0.0 copy-start.3
  31.6 0.6 copy-done.3
  32.2 5.0 %gradient.1 = f32[4,320,128]{2,1,0:T(8,128)} custom-call(s32[1]{0:T(128)} %bitcast.block_ref, s32[2,512]{1,0:T(2,128)} %bitcast.10, s32[512]{0:T(512)} %slot_ref.5, bf16[128,512]{1,0:T(8,128)(2,1)} %copy-done.3, bf16[128,512]{1,0:T(8,128)(2,1)} %bitcast.8, bf16[384,256]{1,0:T(8,128)(2,1)} %get-tuple-element.12.z_ref, f32[384,384]{1,0:T(8,128)} %get-tuple-element.13.e_ref, ...), custom_call_target="tpu_custom_call" | custom-call | tf_op jit(solution)/shard_map/gradient/pallas_call | solution.py:280
  37.2 14.3 %all_to_all.11.got_ref = f32[4,320,128]{2,1,0:T(8,128)} all-to-all(f32[4,320,128]{2,1,0:T(8,128)} %gradient.1), channel_id=1, replica_groups=mesh['blk'=128,'rep'=4] {'rep'}, dimensions={0} | all-to-all | bytes 1310720 | tf_op jit(solution)/shard_map/all_to_all | solution.py:337
  51.5 2.1 %combine.1 = (f32[32,512]{1,0:T(8,128)}, f32[96,512]{1,0:T(8,128)}, f32[96,512]{1,0:T(8,128)}) custom-call(s32[1]{0:T(128)} %bitcast.block_ref, s32[2,512]{1,0:T(2,128)} %bitcast.11, s32[512]{0:T(512)} %slot_ref.5, f32[4,320,128]{2,1,0:T(8,128)} %all_to_all.11.got_ref), custom_call_target="tpu_custom_call" | custom-call | tf_op jit(solution)/shard_map/combine/pallas_call | solution.py:296
  53.6 6.6 %collective-permute-start.2 = (f32[96,512]{1,0:T(8,128)}, f32[96,512]{1,0:T(8,128)S(1)}, u32[]{:S(2)}, u32[]{:S(2)}) collective-permute-start(f32[96,512]{1,0:T(8,128)} %get-tuple-element.18), channel_id=1, source_target_pairs={{0,508},{4,0},{8,4},{12,8},{16,12},{20,16},{24,20},{28,24},{32,28}... | collective-permute-start | bytes 589832 | tf_op jit(solution)/shard_map/ppermute | solution.py:250
  60.2 3.5 %collective-permute-done.2.more_ref = f32[96,512]{1,0:T(8,128)S(1)} collective-permute-done((f32[96,512]{1,0:T(8,128)}, f32[96,512]{1,0:T(8,128)S(1)}, u32[]{:S(2)}, u32[]{:S(2)}) %collective-permute-start.2) | collective-permute-done | bytes 196640 | tf_op jit(solution)/shard_map/ppermute | solution.py:250
  63.7 0.0 copy-start.2
  63.7 0.7 copy-done.2
  64.4 1.7 %total.1 = (f32[64,512]{1,0:T(8,128)}, f32[32,512]{1,0:T(8,128)}) custom-call(f32[96,512]{1,0:T(8,128)} %get-tuple-element.17.own_ref, f32[96,512]{1,0:T(8,128)} %copy-done.2), custom_call_target="tpu_custom_call" | custom-call | tf_op jit(solution)/shard_map/total/pallas_call | solution.py:313
Async XLA Ops:
  0.6 17.6 %collective-permute-start.1 = (bf16[512,256]{1,0:T(8,128)(2,1)}, bf16[512,256]{1,0:T(8,128)(2,1)S(1)}, u32[]{:S(2)}, u32[]{:S(2)}) collective-permute-start(bf16[512,256]{1,0:T(8,128)(2,1)} %own_ref.1), channel_id=1, source_target_pairs={{0,4},{4,8},{8,12},{12,16},{16,20},{20,24},{24,28},{28,32},{32,36}... | collective-permute-start | bytes 786440 | tf_op jit(solution)/shard_map/ppermute | solution.py:250
  16.1 15.4 %copy-start = (bf16[4,32,512]{2,1,0:T(8,128)(2,1)}, bf16[4,32,512]{2,1,0:T(8,128)(2,1)S(1)}, u32[]{:S(2)}) copy-start(bf16[4,32,512]{2,1,0:T(8,128)(2,1)S(1)} %all_to_all.10) | copy-start | bytes 393220
  16.1 15.4 %collective-permute-start = (bf16[128,512]{1,0:T(8,128)(2,1)S(1)}, bf16[128,512]{1,0:T(8,128)(2,1)S(1)}, u32[]{:S(2)}, u32[]{:S(2)}) collective-permute-start(bf16[128,512]{1,0:T(8,128)(2,1)S(1)} %bitcast.7), channel_id=1, source_target_pairs={{0,4},{4,8},{8,12},{12,16},{16,20},{20,24},{24,28},{28,32},{32,36}... | collective-permute-start | bytes 393224 | tf_op jit(solution)/shard_map/ppermute | solution.py:250
  18.2 0.7 %copy-start.1 = (bf16[512,256]{1,0:T(8,128)(2,1)}, bf16[512,256]{1,0:T(8,128)(2,1)S(1)}, u32[]{:S(2)}) copy-start(bf16[512,256]{1,0:T(8,128)(2,1)S(1)} %collective-permute-done.1.prev_ref) | copy-start | bytes 786436
  31.6 0.7 copy-start.3
  53.6 10.1 %collective-permute-start.2 = (f32[96,512]{1,0:T(8,128)}, f32[96,512]{1,0:T(8,128)S(1)}, u32[]{:S(2)}, u32[]{:S(2)}) collective-permute-start(f32[96,512]{1,0:T(8,128)} %get-tuple-element.18), channel_id=1, source_target_pairs={{0,508},{4,0},{8,4},{12,8},{16,12},{20,16},{24,20},{28,24},{32,28}... | collective-permute-start | bytes 589832 | tf_op jit(solution)/shard_map/ppermute | solution.py:250
  63.7 0.7 %copy-start.2 = (f32[96,512]{1,0:T(8,128)}, f32[96,512]{1,0:T(8,128)S(1)}, u32[]{:S(2)}) copy-start(f32[96,512]{1,0:T(8,128)S(1)} %collective-permute-done.2.more_ref) | copy-start | bytes 589828

commit v3 on v2

--- a/solution.py
+++ b/solution.py
@@ -218,11 +218,14 @@
         out_ref[part, zw + tw : zw + 2 * tw, :] = white[part * tw : (part + 1) * tw, :]
 
 
-def combine_kernel(blocks, zw, tw, block_ref, cond_ref, slot_ref, got_ref, white_ref, own_ref, prev_ref):
+def combine_kernel(
+    blocks, zw, tw, block_ref, cond_ref, slot_ref, got_ref, white_ref, z_ref, y_ref, prev_ref
+):
     parts = got_ref.shape[0]
     height = zw + tw
     base = block_ref[0] // blocks * blocks
-    own_ref[...] = jnp.zeros_like(own_ref)
+    z_ref[...] = jnp.zeros_like(z_ref)
+    y_ref[...] = jnp.zeros_like(y_ref)
     prev_ref[...] = jnp.zeros_like(prev_ref)
     for source in range(parts):
         places = member_places(base + source, cond_ref, slot_ref, blocks, None)
@@ -231,7 +234,8 @@
             row = 0 if m == NCOND else height + tw + m * height
             value = got_ref[source, row : row + height, :]
             if m == NCOND:
-                own_ref[:, cols] += value
+                z_ref[:, cols] += value[:zw]
+                y_ref[:, cols] += value[zw:]
                 white_ref[:, cols] = got_ref[source, height : height + tw, :]
             else:
 
@@ -241,7 +245,13 @@
 
                 @pl.when(jnp.logical_not(before))
                 def _():
-                    own_ref[:, cols] += value
+                    z_ref[:, cols] += value[:zw]
+                    y_ref[:, cols] += value[zw:]
+
+
+def near(*values):
+    kept = tuple(pltpu.with_memory_space_constraint(value, pltpu.VMEM) for value in values)
+    return kept if len(kept) > 1 else kept[0]
 
 
 def passed_along(value, axis, steps):
@@ -295,28 +305,11 @@
     rows = blocks * PTS
     return pl.pallas_call(
         functools.partial(combine_kernel, blocks, zw, tw),
-        out_shape=(shape(tw, rows), shape(zw + tw, rows), shape(zw + tw, rows)),
+        out_shape=(shape(tw, rows), shape(zw, rows), shape(tw, rows), shape(zw + tw, rows)),
         in_specs=[SMEM] * 3 + [VMEM],
-        out_specs=(VMEM,) * 3,
+        out_specs=(VMEM,) * 4,
         name="combine",
     )(block, cond, slots, got)
-
-
-def sum_kernel(own_ref, more_ref, z_ref, y_ref):
-    zw = z_ref.shape[0]
-    z_ref[...] = own_ref[:zw, :] + more_ref[:zw, :]
-    y_ref[...] = own_ref[zw:, :] + more_ref[zw:, :]
-
-
-def sum_call(parts, own, more):
-    rows = own.shape[1]
-    return pl.pallas_call(
-        sum_kernel,
-        out_shape=(shape(F // parts, rows), shape(T_SIZE // parts, rows)),
-        in_specs=[VMEM] * 2,
-        out_specs=(VMEM,) * 2,
-        name="total",
-    )(own, more)
 
 
 def per_device(features, targets, conditioning, block_slot):
@@ -324,20 +317,21 @@
     blocks = features.shape[0] // PTS
     block = (lax.axis_index("blk") * blocks + lax.axis_index("rep")).astype(jnp.int32)[None]
     cond = conditioning.T
-    prev_features = passed_along(features, "blk", 1)
+    prev_features = near(passed_along(features, "blk", 1))
     columns = targets.T
     gathered = lax.all_to_all(
         jnp.broadcast_to(columns[None], (parts,) + columns.shape), "rep", 0, 0, tiled=True
     ).reshape(T_SIZE, features.shape[0])
-    prev_targets = passed_along(gathered, "blk", 1)
+    prev_targets = near(passed_along(gathered, "blk", 1))
     z, e, la, p = factor_call(blocks, block, cond, block_slot, prev_features, features)
     sent = gradient_call(
         blocks, parts, block, cond, block_slot, prev_targets, gathered, z, e, la, p
     )
     got = lax.all_to_all(sent, "rep", 0, 0, tiled=True)
-    white, own, prev = combine_call(blocks, parts, block, cond, block_slot, got)
-    grad_z, grad_y = sum_call(parts, own, passed_along(prev, "blk", -1))
-    return (white.T, grad_z.T, grad_y.T)
+    white, own_z, own_y, prev = combine_call(blocks, parts, block, cond, block_slot, got)
+    more = passed_along(prev, "blk", -1)
+    zw = F // parts
+    return (white.T, (own_z + more[:zw]).T, (own_y + more[zw:]).T)
 
 
 def solution(mesh):

time: 66.6 us -> 65.4 us (0.982)
  other arithmetic: 0 us -> 2.15 us
  local copies, waits for them, and re-layouts: 2.78 us -> 0.78 us
  Pallas kernels: 21.4 us -> 19.8 us
    transpose x0 -> x2, other arithmetic: none -> 2.15 us  [per_device(): return (white.T, (own_z + more[:zw]).T, (own_y + more[zw:]).T)]
    unnamed x8 -> x4, local copies, waits for them, and re-layouts: 2.01 us -> 0.01 us
    pallas_call x1 -> x0, Pallas kernels: 1.71 us -> none  [sum_call(): pl.pallas_call(sum_kernel, out_shape=(shape(F // parts, rows), shape(T_SI...]
  transfers between devices with their start and end apart: 3 -> 3, of which waited for: 2 -> 2; matrix products, arithmetic and copies ran while one was open for 1% -> 1% of each run, Pallas kernels for 19% -> 20%
where the time goes in v3:
time: 65.4 us; the launch traced here: 64.8 us
  blocking collectives  27.1 us (41%)
  Pallas kernels  19.8 us (30%)
  starting transfers between devices  10.6 us (16%)
  waiting for transfers between devices  3.63 us (6%)
  other arithmetic  2.15 us (3%)
  local copies, waits for them, and re-layouts  0.78 us (1%)
  between operations  0.7 us (1%)
    all_to_all x1, blocking collectives, per_device(): got = lax.all_to_all(sent, 'rep', 0, 0, tiled=True)  14.4 us
    all_to_all x1, blocking collectives, per_device(): lax.all_to_all(jnp.broadcast_to(columns[None], (parts,) + columns.shape),...  12.8 us
    pallas_call x1, Pallas kernels, factor_call(): pl.pallas_call(functools.partial(factor_kernel, blocks), out_shape=(shape...  12.7 us
    ppermute x3, starting transfers between devices, passed_along(): return lax.ppermute(value, axis, pairs)  10.6 us
    pallas_call x1, Pallas kernels, gradient_call(): pl.pallas_call(functools.partial(gradient_kernel, blocks), out_shape=shap...  5.01 us
    ppermute x3, waiting for transfers between devices, passed_along(): return lax.ppermute(value, axis, pairs)  3.63 us
    transpose x2, other arithmetic, per_device(): return (white.T, (own_z + more[:zw]).T, (own_y + more[zw:]).T)  2.15 us
    pallas_call x1, Pallas kernels, combine_call(): pl.pallas_call(functools.partial(combine_kernel, blocks, zw, tw), out_sha...  2.08 us
  transfers between devices with their start and end apart: 3, of which 2 were waited for; matrix products, arithmetic and copies ran while one was open for 1% of the time, Pallas kernels for 20%

profile of v3, /device:TPU:2, one launch (start us, length us, event | category | flops | bytes accessed | tf_op | source)
XLA Modules:
  0.0 64.8 jit_solution(11083854166624978130)
XLA Ops:
  0.6 1.9 %collective-permute-start.1 = (bf16[512,256]{1,0:T(8,128)(2,1)}, bf16[512,256]{1,0:T(8,128)(2,1)S(1)}, u32[]{:S(2)}, u32[]{:S(2)}) collective-permute-start(bf16[512,256]{1,0:T(8,128)(2,1)} %own_ref.1), channel_id=1, source_target_pairs={{0,4},{4,8},{8,12},{12,16},{16,20},{20,24},{24,28},{28,32},{32,36}... | collective-permute-start | bytes 786440 | tf_op jit(solution)/shard_map/ppermute | solution.py:260
  2.6 0.8 %broadcast_in_dim.10 = bf16[4,32,512]{2,1,0:T(8,128)(2,1)S(1)} broadcast(bf16[32,512]{1,0:T(8,128)(2,1)} %bitcast.14), dimensions={1,2} | broadcast | bytes 163840 | tf_op jit(solution)/shard_map/broadcast_in_dim | solution.py:323
  3.3 12.8 %all_to_all.10 = bf16[4,32,512]{2,1,0:T(8,128)(2,1)S(1)} all-to-all(bf16[4,32,512]{2,1,0:T(8,128)(2,1)S(1)} %broadcast_in_dim.10), channel_id=1, replica_groups=mesh['blk'=128,'rep'=4] {'rep'}, dimensions={0} | all-to-all | bytes 262144 | tf_op jit(solution)/shard_map/all_to_all | solution.py:322
  16.1 0.0 copy-start
  16.1 1.9 %collective-permute-start = (bf16[128,512]{1,0:T(8,128)(2,1)S(1)}, bf16[128,512]{1,0:T(8,128)(2,1)S(1)}, u32[]{:S(2)}, u32[]{:S(2)}) collective-permute-start(bf16[128,512]{1,0:T(8,128)(2,1)S(1)} %bitcast.9), channel_id=1, source_target_pairs={{0,4},{4,8},{8,12},{12,16},{16,20},{20,24},{24,28},{28,32},{32,36}... | collective-permute-start | bytes 393224 | tf_op jit(solution)/shard_map/ppermute | solution.py:260
  18.0 0.1 collective-permute-done.1.prev_ref
  18.2 12.7 %factor.1 = (bf16[384,256]{1,0:T(8,128)(2,1)}, f32[384,384]{1,0:T(8,128)}, f32[256,256]{1,0:T(8,128)}, f32[128,384]{1,0:T(8,128)}) custom-call(s32[1]{0:T(128)} %bitcast.block_ref, s32[2,512]{1,0:T(2,128)} %bitcast.11, s32[512]{0:T(512)} %slot_ref.5, bf16[512,256]{1,0:T(8,128)(2,1)S(1)} %collective-permute-done.1.prev_ref, bf16[512,256]{1,0:T(8,128)(2,1)} %own_ref.1), custom_call_target="tpu_custom_call" | custom-call | tf_op jit(solution)/shard_map/factor/pallas_call | solution.py:273
  30.9 0.0 copy-done
  30.9 0.0 collective-permute-done.prev_ref
  30.9 5.0 %gradient.1 = f32[4,320,128]{2,1,0:T(8,128)} custom-call(s32[1]{0:T(128)} %bitcast.block_ref, s32[2,512]{1,0:T(2,128)} %bitcast.12, s32[512]{0:T(512)} %slot_ref.5, bf16[128,512]{1,0:T(8,128)(2,1)S(1)} %collective-permute-done.prev_ref, bf16[128,512]{1,0:T(8,128)(2,1)} %bitcast.10, bf16[384,256]{1,0:T(8,128)(2,1)} %get-tuple-element.11.z_ref, ...), custom_call_target="tpu_custom_call" | custom-call | tf_op jit(solution)/shard_map/gradient/pallas_call | solution.py:290
  35.9 14.4 %all_to_all.11.got_ref = f32[4,320,128]{2,1,0:T(8,128)} all-to-all(f32[4,320,128]{2,1,0:T(8,128)} %gradient.1), channel_id=1, replica_groups=mesh['blk'=128,'rep'=4] {'rep'}, dimensions={0} | all-to-all | bytes 1310720 | tf_op jit(solution)/shard_map/all_to_all | solution.py:330
  50.3 2.1 %combine.1 = (f32[32,512]{1,0:T(8,128)}, f32[64,512]{1,0:T(8,128)}, f32[32,512]{1,0:T(8,128)}, f32[96,512]{1,0:T(8,128)}) custom-call(s32[1]{0:T(128)} %bitcast.block_ref, s32[2,512]{1,0:T(2,128)} %bitcast.13, s32[512]{0:T(512)} %slot_ref.5, f32[4,320,128]{2,1,0:T(8,128)} %all_to_all.11.got_ref), custom_call_target="tpu_custom_call" | custom-call | tf_op jit(solution)/shard_map/combine/pallas_call | solution.py:306
  52.4 0.0 copy-start.1
  52.4 6.8 %collective-permute-start.2 = (f32[96,512]{1,0:T(8,128)}, f32[96,512]{1,0:T(8,128)S(1)}, u32[]{:S(2)}, u32[]{:S(2)}) collective-permute-start(f32[96,512]{1,0:T(8,128)} %get-tuple-element.17), channel_id=1, source_target_pairs={{0,508},{4,0},{8,4},{12,8},{16,12},{20,16},{24,20},{28,24},{32,28}... | collective-permute-start | bytes 589832 | tf_op jit(solution)/shard_map/ppermute | solution.py:260
  59.1 3.5 %collective-permute-done.2 = f32[96,512]{1,0:T(8,128)S(1)} collective-permute-done((f32[96,512]{1,0:T(8,128)}, f32[96,512]{1,0:T(8,128)S(1)}, u32[]{:S(2)}, u32[]{:S(2)}) %collective-permute-start.2) | collective-permute-done | bytes 196640 | tf_op jit(solution)/shard_map/ppermute | solution.py:260
  62.6 1.5 %fusion.1 = f32[512,32]{0,1:T(8,128)} fusion(f32[32,512]{1,0:T(8,128)} %get-tuple-element.18, f32[96,512]{1,0:T(8,128)S(1)} %collective-permute-done.2), kind=kLoop, calls=%fused_computation.3 | loop fusion | flops 16384 | bytes 196608 | tf_op jit(solution)/shard_map/transpose | solution.py:334
  64.1 0.0 copy-done.1
  64.1 0.7 %fusion = f32[512,64]{0,1:T(8,128)} fusion(f32[64,512]{1,0:T(8,128)S(1)} %copy-done.1, f32[96,512]{1,0:T(8,128)S(1)} %collective-permute-done.2), kind=kLoop, calls=%fused_computation.1 | loop fusion | flops 32768 | bytes 393216 | tf_op jit(solution)/shard_map/transpose | solution.py:334
Async XLA Ops:
  0.6 17.6 %collective-permute-start.1 = (bf16[512,256]{1,0:T(8,128)(2,1)}, bf16[512,256]{1,0:T(8,128)(2,1)S(1)}, u32[]{:S(2)}, u32[]{:S(2)}) collective-permute-start(bf16[512,256]{1,0:T(8,128)(2,1)} %own_ref.1), channel_id=1, source_target_pairs={{0,4},{4,8},{8,12},{12,16},{16,20},{20,24},{24,28},{28,32},{32,36}... | collective-permute-start | bytes 786440 | tf_op jit(solution)/shard_map/ppermute | solution.py:260
  16.1 14.8 %copy-start = (bf16[4,32,512]{2,1,0:T(8,128)(2,1)}, bf16[4,32,512]{2,1,0:T(8,128)(2,1)S(1)}, u32[]{:S(2)}) copy-start(bf16[4,32,512]{2,1,0:T(8,128)(2,1)S(1)} %all_to_all.10) | copy-start | bytes 393220
  16.1 14.8 %collective-permute-start = (bf16[128,512]{1,0:T(8,128)(2,1)S(1)}, bf16[128,512]{1,0:T(8,128)(2,1)S(1)}, u32[]{:S(2)}, u32[]{:S(2)}) collective-permute-start(bf16[128,512]{1,0:T(8,128)(2,1)S(1)} %bitcast.9), channel_id=1, source_target_pairs={{0,4},{4,8},{8,12},{12,16},{16,20},{20,24},{24,28},{28,32},{32,36}... | collective-permute-start | bytes 393224 | tf_op jit(solution)/shard_map/ppermute | solution.py:260
  52.4 11.7 %copy-start.1 = (f32[64,512]{1,0:T(8,128)S(1)}, f32[64,512]{1,0:T(8,128)}, u32[]{:S(2)}) copy-start(f32[64,512]{1,0:T(8,128)} %get-tuple-element.16) | copy-start | bytes 393220
  52.4 10.2 %collective-permute-start.2 = (f32[96,512]{1,0:T(8,128)}, f32[96,512]{1,0:T(8,128)S(1)}, u32[]{:S(2)}, u32[]{:S(2)}) collective-permute-start(f32[96,512]{1,0:T(8,128)} %get-tuple-element.17), channel_id=1, source_target_pairs={{0,508},{4,0},{8,4},{12,8},{16,12},{20,16},{24,20},{28,24},{32,28}... | collective-permute-start | bytes 589832 | tf_op jit(solution)/shard_map/ppermute | solution.py:260
